TPU v7x, 32 devices: a whole 2x2x4 slice. The times are simulated.
32 devices in a mesh: groups: 2 (over y), samp: 4 (over z), feat: 4 (over x, core).
Axes of the slice: x: 2, y: 2, z: 4, core: 2. Of those that a mesh axis runs over, the one named last changes fastest.
Arguments:
- x_blocks: bfloat16 [64, 64, 128, 128], P(('groups', 'samp'), 'feat'), parts along dimension 0, may hold values from -6 to 6
- block_cols: int32 [64, 64], P('groups', 'feat'), parts along dimension 0, may hold values from 0 to 31
- labels: int32 [8192], P('groups'), parts along dimension 0, may hold values from 0 to 63
- group_ids: int32 [8192], P('groups'), parts along dimension 0, may hold values from 0 to 7, as said below
- picks: int32 [3, 32], P(None, 'groups'), parts along dimension 1, may hold values from 0 to 31, as said below
- w_init: float32 [16384, 64], P('feat'), may hold values from -2.253903 to 2.253903
Outputs:
- scores: float32 [8192, 64], P(('groups', 'samp')), parts along dimension 0
- adversary: float32 [16], P('groups'), parts along dimension 0
There are 2 independent parts, one for each index of `groups`. A program takes and returns all parts, laid end to end along the dimension named above; an argument that names none is the same for every part. Nothing has to cross between parts.
Inputs may be any that keep to these rules, and one draw needn't show every extreme that they name: `group_ids`: every row block of 128 samples holds every group at least once. `picks`: the entries of one step are distinct. Row block b is owned by index b // 8 of samp. The k-th aligned block of 4 entries of a step is the list of index k of samp; it names row blocks owned by index k or by the next index along samp (index 0 after the last); between one and 2 entries of each list name the next index's row blocks, exactly 2 in at least one list of every step.
All inputs are finite; a program needn't handle non-finite values.
Results may differ from a plain program's by a relative error of at most 0.00315.
The roundings to bfloat16 on the way count: a program that leaves them out, or rounds other values in their place, can miss the bound.
Values may be sent and summed in bfloat16 or wider, within the bound.
No kernel may reach another device: no remote copies, remote signals or barrier semaphores. Data moves between devices by JAX's collectives and lax.ppermute only.
A program may use at most 64 MiB of HBM per device.

v0:
```python
import jax
import jax.numpy as jnp
from jax import lax
from jax.sharding import PartitionSpec as P

GRP = 8
STEPS = 3
weight_rate = 8.0
adv_rate = 2.0


def per_device(x_blocks, block_cols, labels, group_ids, picks, w_init):
    row_blocks, per_row, block_size, _ = x_blocks.shape
    feat_rows, classes = w_init.shape
    col_blocks = feat_rows // block_size
    total_blocks = block_cols.shape[0]
    feat_count = lax.axis_size("feat")
    my_index = lax.axis_index("samp")
    step_rate = weight_rate * picks.shape[1] / (per_row * feat_count)
    class_range = jnp.arange(classes, dtype=jnp.int32)
    group_range = jnp.arange(GRP, dtype=jnp.int32)
    block_range = jnp.arange(total_blocks, dtype=jnp.int32)
    col_range = jnp.arange(col_blocks, dtype=jnp.int32)
    sample_groups = (group_ids[:, None] == group_range[None, :]).astype(jnp.float32)
    block_groups = jnp.sum(sample_groups.reshape(total_blocks, block_size, GRP), axis=1)
    own_start = my_index * row_blocks
    own_cols = lax.dynamic_slice_in_dim(block_cols, own_start, row_blocks, 0)
    own_labels = lax.dynamic_slice_in_dim(
        labels, own_start * block_size, row_blocks * block_size, 0
    )
    own_groups = lax.dynamic_slice_in_dim(
        group_ids, own_start * block_size, row_blocks * block_size, 0
    )

    def total_logits(x_rows, col_rows, weights_bf):
        tiles = weights_bf.reshape(col_blocks, block_size, classes)[col_rows]
        partial_sum = jnp.einsum(
            "rbij,rbjc->ric", x_rows, tiles, preferred_element_type=jnp.float32
        )
        summed = lax.psum(partial_sum, "feat")
        return summed.reshape(-1, classes)

    def evaluate(row_data, weights_bf, adversary, counts):
        x_rows, col_rows, label_rows, group_rows, mult_rows = row_data
        logits = total_logits(x_rows, col_rows, weights_bf)
        label_hot = (label_rows[:, None] == class_range[None, :]).astype(jnp.float32)
        group_hot = (group_rows[:, None] == group_range[None, :]).astype(jnp.float32)
        log_total = jax.nn.logsumexp(logits, axis=-1)
        cross = log_total - jnp.sum(logits * label_hot, axis=-1)
        probs = jnp.exp(logits - log_total[:, None])
        local_loss = jnp.dot(mult_rows * cross, group_hot, precision=lax.Precision.HIGHEST)
        loss = lax.psum(local_loss, "samp") / counts
        coef = jnp.dot(group_hot, adversary / counts, precision=lax.Precision.HIGHEST) * mult_rows
        dz_rows = (coef[:, None] * (probs - label_hot)).astype(jnp.bfloat16)
        blocks_here = x_rows.shape[0]
        dz_blocks = dz_rows.reshape(blocks_here, block_size, classes)
        grad_tiles = jnp.einsum(
            "rbij,ric->rbjc", x_rows, dz_blocks, preferred_element_type=jnp.float32
        )
        grad_tiles = grad_tiles.reshape(blocks_here * per_row, block_size * classes)
        col_hot = (col_rows.reshape(-1)[:, None] == col_range[None, :]).astype(jnp.float32)
        grad_local = jnp.dot(col_hot.T, grad_tiles, precision=lax.Precision.HIGHEST)
        return (loss, grad_local.reshape(feat_rows, classes))

    def advance(state, grad_local):
        grad_total = lax.psum(grad_local, "samp")
        new_state = state - step_rate * grad_total
        return (new_state, new_state.astype(jnp.bfloat16))

    state = w_init
    weights_bf = w_init.astype(jnp.bfloat16)
    adversary = jnp.full((GRP,), 1.0 / GRP, jnp.float32)
    for step in range(STEPS):
        block_hits = jnp.sum(
            (picks[step][:, None] == block_range[None, :]).astype(jnp.float32), axis=0
        )
        counts = jnp.dot(block_hits, block_groups, precision=lax.Precision.HIGHEST)
        own_hits = lax.dynamic_slice_in_dim(block_hits, own_start, row_blocks, 0)
        row_data = (x_blocks, own_cols, own_labels, own_groups, jnp.repeat(own_hits, block_size))
        loss_first, grad_first = evaluate(row_data, weights_bf, adversary, counts)
        half_state, half_bf = advance(state, grad_first)
        half_adv = jax.nn.softmax(jnp.log(adversary) + adv_rate * loss_first)
        loss_second, grad_second = evaluate(row_data, half_bf, half_adv, counts)
        state, weights_bf = advance(state, grad_second)
        adversary = jax.nn.softmax(jnp.log(adversary) + adv_rate * loss_second)
    return (total_logits(x_blocks, own_cols, weights_bf), adversary)


def solution(mesh):
    in_specs = (
        P(("groups", "samp"), "feat", None, None),
        P("groups", "feat"),
        P("groups"),
        P("groups"),
        P(None, "groups"),
        P("feat", None),
    )
    out_specs = (P(("groups", "samp"), None), P("groups"))
    return jax.shard_map(
        per_device, mesh=mesh, in_specs=in_specs, out_specs=out_specs, check_vma=False
    )
```

profile of v0, /device:TPU:0, one launch (start us, length us, event | category | flops | bytes accessed | tf_op | source)
XLA Modules:
  0.0 842.0 jit_solution(14522523979013200713)
XLA Ops:
  10.5 4.4 convolution_bitcast_fusion.12
  16.2 33.7 %all-reduce.17.cloned.1.call-done = f32[8,128,64]{1,2,0:T(8,128)} async-done(((f32[8,128,64]{1,2,0:T(8,128)}), f32[8,128,64]{1,2,0:T(8,128)}) %all-reduce.17.cloned.1.call-update) | async-done | bytes 262160 | tf_op jit(solution)/shard_map/psum | solution.py:40
  51.9 5.0 convolution_bitcast_fusion.5
  56.8 6.9 copy.85
  63.7 7.9 reshape.440
  71.6 3.8 fusion.69
  75.5 2.2 reshape.441
  77.6 3.2 copy.86
  80.9 51.9 %all-reduce.19.cloned.1.call-done = f32[4096,64]{0,1:T(8,128)} async-done(((f32[4096,64]{0,1:T(8,128)}), f32[4096,64]{0,1:T(8,128)}) %all-reduce.19.cloned.1.call-update) | async-done | bytes 1048592 | tf_op jit(solution)/shard_map/psum | solution.py:66
  134.2 2.2 gather_fusion.1
  136.4 5.1 convolution_bitcast_fusion.11
  141.5 31.5 %all-reduce.21.cloned.1.call-done = f32[8,128,64]{1,2,0:T(8,128)} async-done(((f32[8,128,64]{1,2,0:T(8,128)}), f32[8,128,64]{1,2,0:T(8,128)}) %all-reduce.21.cloned.1.call-update) | async-done | bytes 262160 | tf_op jit(solution)/shard_map/psum | solution.py:40
  175.8 12.2 %all-reduce.2 = (f32[8]{0:T(128)S(1)}, f32[8]{0:T(128)S(1)}) all-reduce(f32[8]{0:T(128)S(1)} %convolution_bitcast_fusion.21, f32[8]{0:T(128)S(1)} %convolution_bitcast_fusion.20), channel_id=1, replica_groups=mesh['groups'=2,'samp'=4,'feat'=4] {'samp'}, use_global_device_ids=true, to_apply=%region_5.0 | all-reduce | flops 16 | bytes 128 | tf_op jit(solution)/shard_map/psum | solution.py:52
  188.6 2.0 fusion.117
  192.4 5.0 convolution_bitcast_fusion.4
  197.3 6.9 copy.88
  204.2 7.9 reshape.443
  212.1 3.8 fusion.68
  215.9 2.2 reshape.444
  218.1 3.2 copy.89
  223.3 47.3 %all-reduce.23.cloned.1.call-done = f32[4096,64]{0,1:T(8,128)} async-done(((f32[4096,64]{0,1:T(8,128)}), f32[4096,64]{0,1:T(8,128)}) %all-reduce.23.cloned.1.call-update) | async-done | bytes 1048592 | tf_op jit(solution)/shard_map/psum | solution.py:66
  272.0 2.2 gather_fusion.2
  274.1 5.1 convolution_bitcast_fusion.10
  279.3 31.4 %all-reduce.25.cloned.1.call-done = f32[8,128,64]{1,2,0:T(8,128)} async-done(((f32[8,128,64]{1,2,0:T(8,128)}), f32[8,128,64]{1,2,0:T(8,128)}) %all-reduce.25.cloned.1.call-update) | async-done | bytes 262160 | tf_op jit(solution)/shard_map/psum | solution.py:40
  312.8 5.0 convolution_bitcast_fusion.3
  317.7 6.9 copy.91
  324.6 7.9 reshape.447
  332.5 4.8 fusion.67
  337.3 3.2 reshape.448
  340.5 3.2 copy.92
  344.0 51.8 %all-reduce.27.cloned.1.call-done = f32[4096,64]{0,1:T(8,128)} async-done(((f32[4096,64]{0,1:T(8,128)}), f32[4096,64]{0,1:T(8,128)}) %all-reduce.27.cloned.1.call-update) | async-done | bytes 1048592 | tf_op jit(solution)/shard_map/psum | solution.py:66
  397.1 2.2 gather_fusion.3
  399.3 5.1 convolution_bitcast_fusion.9
  404.4 31.4 %all-reduce.29.cloned.1.call-done = f32[8,128,64]{1,2,0:T(8,128)} async-done(((f32[8,128,64]{1,2,0:T(8,128)}), f32[8,128,64]{1,2,0:T(8,128)}) %all-reduce.29.cloned.1.call-update) | async-done | bytes 262160 | tf_op jit(solution)/shard_map/psum | solution.py:40
  438.7 11.7 %all-reduce.1 = (f32[8]{0:T(128)S(1)}, f32[8]{0:T(128)S(1)}) all-reduce(f32[8]{0:T(128)S(1)} %convolution_bitcast_fusion.19, f32[8]{0:T(128)S(1)} %convolution_bitcast_fusion.18), channel_id=1, replica_groups=mesh['groups'=2,'samp'=4,'feat'=4] {'samp'}, use_global_device_ids=true, to_apply=%region_23.0 | all-reduce | flops 16 | bytes 128 | tf_op jit(solution)/shard_map/psum | solution.py:52
  455.9 5.0 convolution_bitcast_fusion.2
  460.9 6.9 copy.94
  467.8 7.9 reshape.450
  475.7 4.8 fusion.66
  480.5 3.1 reshape.451
  483.6 3.2 copy.95
  490.0 46.1 %all-reduce.31.cloned.1.call-done = f32[4096,64]{0,1:T(8,128)} async-done(((f32[4096,64]{0,1:T(8,128)}), f32[4096,64]{0,1:T(8,128)}) %all-reduce.31.cloned.1.call-update) | async-done | bytes 1048592 | tf_op jit(solution)/shard_map/psum | solution.py:66
  536.1 2.5 convert_bitcast_fusion
  539.6 4.4 convolution_bitcast_fusion.8
  544.4 31.2 %all-reduce.33.cloned.1.call-done = f32[8,128,64]{1,2,0:T(8,128)} async-done(((f32[8,128,64]{1,2,0:T(8,128)}), f32[8,128,64]{1,2,0:T(8,128)}) %all-reduce.33.cloned.1.call-update) | async-done | bytes 262160 | tf_op jit(solution)/shard_map/psum | solution.py:40
  577.7 5.0 convolution_bitcast_fusion.1
  582.7 6.9 copy.97
  589.6 7.9 reshape.454
  597.5 3.8 fusion.65
  601.3 2.2 reshape.455
  603.5 3.2 copy.98
  606.7 51.9 %all-reduce.35.cloned.1.call-done = f32[4096,64]{0,1:T(8,128)} async-done(((f32[4096,64]{0,1:T(8,128)}), f32[4096,64]{0,1:T(8,128)}) %all-reduce.35.cloned.1.call-update) | async-done | bytes 1048592 | tf_op jit(solution)/shard_map/psum | solution.py:66
  661.0 4.4 convolution_bitcast_fusion.7
  665.5 31.5 %all-reduce.37.cloned.1.call-done = f32[8,128,64]{1,2,0:T(8,128)} async-done(((f32[8,128,64]{1,2,0:T(8,128)}), f32[8,128,64]{1,2,0:T(8,128)}) %all-reduce.37.cloned.1.call-update) | async-done | bytes 262160 | tf_op jit(solution)/shard_map/psum | solution.py:40
  699.8 11.7 %all-reduce = (f32[8]{0:T(128)S(1)}, f32[8]{0:T(128)S(1)}) all-reduce(f32[8]{0:T(128)S(1)} %convolution_bitcast_fusion.17, f32[8]{0:T(128)S(1)} %convolution_bitcast_fusion.16), channel_id=1, replica_groups=mesh['groups'=2,'samp'=4,'feat'=4] {'samp'}, use_global_device_ids=true, to_apply=%region_40.0 | all-reduce | flops 16 | bytes 128 | tf_op jit(solution)/shard_map/psum | solution.py:52
  717.0 5.0 convolution_bitcast_fusion
  722.0 6.9 copy.100
  728.9 7.9 reshape.457
  736.8 3.8 fusion.64
  740.6 2.2 reshape.458
  742.8 3.2 copy.101
  747.3 47.9 %all-reduce.39.cloned.1.call-done = f32[4096,64]{0,1:T(8,128)} async-done(((f32[4096,64]{0,1:T(8,128)}), f32[4096,64]{0,1:T(8,128)}) %all-reduce.39.cloned.1.call-update) | async-done | bytes 1048592 | tf_op jit(solution)/shard_map/psum | solution.py:66
  797.6 3.7 convolution_bitcast_fusion.6
  803.8 29.7 %all-reduce.41.cloned.1.call-done = f32[1024,64]{0,1:T(8,128)} async-done(((f32[1024,64]{0,1:T(8,128)}), f32[1024,64]{0,1:T(8,128)}) %all-reduce.41.cloned.1.call-update) | async-done | bytes 262160 | tf_op jit(solution)/shard_map/psum | solution.py:40
  (129 shorter events, 54.0 us)
Async XLA Ops:
  7.2 9.0 %copy-start = (s32[4096]{0:T(1024)S(1)}, s32[4096]{0:T(1024)}, u32[]{:S(2)}) copy-start(s32[4096]{0:T(1024)} %param.8) | copy-start | bytes 49156
  7.2 42.6 %all-reduce.17.cloned.1.call-start = ((), (), s32[]{:S(2)}) async-start(), calls=%async_computation | async-start | bytes 524288 | tf_op jit(solution)/shard_map/psum | solution.py:40
  10.5 4.5 copy-start.7
  10.5 4.7 copy-start.6
  15.0 117.8 %all-reduce.19.cloned.1.call-start = ((), (), s32[]{:S(2)}) async-start(), calls=%async_computation.1 | async-start | bytes 2097152 | tf_op jit(solution)/shard_map/psum | solution.py:66
  75.4 57.4 %copy-start.2 = (f32[4096,64]{0,1:T(8,128)S(1)}, f32[4096,64]{0,1:T(8,128)}, u32[]{:S(2)}) copy-start(f32[4096,64]{0,1:T(8,128)} %param.11) | copy-start | bytes 3145732
  80.8 92.1 %all-reduce.21.cloned.1.call-start = ((), (), s32[]{:S(2)}) async-start(), calls=%async_computation.2 | async-start | bytes 524288 | tf_op jit(solution)/shard_map/psum | solution.py:40
  141.4 129.2 %all-reduce.23.cloned.1.call-start = ((), (), s32[]{:S(2)}) async-start(), calls=%async_computation.3 | async-start | bytes 2097152 | tf_op jit(solution)/shard_map/psum | solution.py:66
  221.3 89.4 %all-reduce.25.cloned.1.call-start = ((), (), s32[]{:S(2)}) async-start(), calls=%async_computation.4 | async-start | bytes 524288 | tf_op jit(solution)/shard_map/psum | solution.py:40
  279.2 116.5 %all-reduce.27.cloned.1.call-start = ((), (), s32[]{:S(2)}) async-start(), calls=%async_computation.5 | async-start | bytes 2097152 | tf_op jit(solution)/shard_map/psum | solution.py:66
  337.3 58.4 %copy-start.3 = (f32[4096,64]{0,1:T(8,128)S(1)}, f32[4096,64]{0,1:T(8,128)}, u32[]{:S(2)}) copy-start(f32[4096,64]{0,1:T(8,128)} %all-reduce.23.cloned.1.call-done) | copy-start | bytes 3145732
  343.7 92.1 %all-reduce.29.cloned.1.call-start = ((), (), s32[]{:S(2)}) async-start(), calls=%async_computation.6 | async-start | bytes 524288 | tf_op jit(solution)/shard_map/psum | solution.py:40
  404.4 131.7 %all-reduce.31.cloned.1.call-start = ((), (), s32[]{:S(2)}) async-start(), calls=%async_computation.7 | async-start | bytes 2097152 | tf_op jit(solution)/shard_map/psum | solution.py:66
  486.8 88.9 %all-reduce.33.cloned.1.call-start = ((), (), s32[]{:S(2)}) async-start(), calls=%async_computation.8 | async-start | bytes 524288 | tf_op jit(solution)/shard_map/psum | solution.py:40
  544.1 114.6 %all-reduce.35.cloned.1.call-start = ((), (), s32[]{:S(2)}) async-start(), calls=%async_computation.9 | async-start | bytes 2097152 | tf_op jit(solution)/shard_map/psum | solution.py:66
  601.3 57.4 %copy-start.4 = (f32[4096,64]{0,1:T(8,128)S(1)}, f32[4096,64]{0,1:T(8,128)}, u32[]{:S(2)}) copy-start(f32[4096,64]{0,1:T(8,128)} %get-tuple-element.29) | copy-start | bytes 3145732
  606.7 90.3 %all-reduce.37.cloned.1.call-start = ((), (), s32[]{:S(2)}) async-start(), calls=%async_computation.10 | async-start | bytes 524288 | tf_op jit(solution)/shard_map/psum | solution.py:40
  665.4 129.8 %all-reduce.39.cloned.1.call-start = ((), (), s32[]{:S(2)}) async-start(), calls=%async_computation.11 | async-start | bytes 2097152 | tf_op jit(solution)/shard_map/psum | solution.py:66
  740.6 54.6 %copy-start.5 = (f32[4096,64]{0,1:T(8,128)S(1)}, f32[4096,64]{0,1:T(8,128)}, u32[]{:S(2)}) copy-start(f32[4096,64]{0,1:T(8,128)} %get-tuple-element.29) | copy-start | bytes 3145732
  746.0 87.6 %all-reduce.41.cloned.1.call-start = ((), (), s32[]{:S(2)}) async-start(), calls=%async_computation.12 | async-start | bytes 524288 | tf_op jit(solution)/shard_map/psum | solution.py:40
  796.6 38.6 %copy-start.1 = (s32[4096]{0:T(1024)S(1)}, s32[4096]{0:T(1024)}, u32[]{:S(2)}) copy-start(s32[4096]{0:T(1024)} %param.8) | copy-start | bytes 49156
Sparse Core Ops, SparseCore 0:
  15.1 34.6 all-reduce.16
  80.9 51.8 all-reduce.18
  141.6 31.3 all-reduce.20
  221.4 49.1 all-reduce.22
  279.3 31.3 all-reduce.24
  343.9 51.8 all-reduce.26
  404.5 31.3 all-reduce.28
  486.9 49.1 all-reduce.30
  544.2 31.4 all-reduce.32
  606.8 51.8 all-reduce.34
  665.5 31.3 all-reduce.36
  746.1 49.0 all-reduce.38
  802.2 31.3 all-reduce.40
where the time goes:
time: 851 us; the launch traced here: 842 us
  waiting for transfers between devices  518 us (61%)
  local copies, waits for them, and re-layouts  136 us (16%)
  matrix products  98.5 us (12%)
  other arithmetic  38.8 us (5%)
  blocking collectives  35.5 us (4%)
  between operations  14.6 us (2%)
    psum x6, waiting for transfers between devices, advance(): grad_total = lax.psum(grad_local, 'samp')  297 us
    psum x7, waiting for transfers between devices, total_logits(): summed = lax.psum(partial_sum, 'feat')  220 us
    reshape x6, local copies, waits for them, and re-layouts, evaluate(): grad_tiles = grad_tiles.reshape(blocks_here * per_row, block_size * classes)  47.3 us
    dot_general x6, local copies, waits for them, and re-layouts, evaluate(): jnp.einsum('rbij,ric->rbjc', x_rows, dz_blocks, preferred_element_type=jn...  41.4 us
    psum x3, blocking collectives, evaluate(): loss = lax.psum(local_loss, 'samp') / counts  35.5 us
    reshape x12, local copies, waits for them, and re-layouts, evaluate(): return (loss, grad_local.reshape(feat_rows, classes))  34.1 us
    dot_general x7, matrix products, total_logits(): jnp.einsum('rbij,rbjc->ric', x_rows, tiles, preferred_element_type=jnp.fl...  32.2 us
    dot_general x6, matrix products, evaluate(): jnp.einsum('rbij,ric->rbjc', x_rows, dz_blocks, preferred_element_type=jn...  29.8 us
  transfers between devices with their start and end apart: 13, of which 13 were waited for; matrix products, arithmetic and copies ran while one was open for 1% of the time, Pallas kernels for 0%

commit v1 on v0

--- a/solution.py
+++ b/solution.py
@@ -37,7 +37,7 @@
         partial_sum = jnp.einsum(
             "rbij,rbjc->ric", x_rows, tiles, preferred_element_type=jnp.float32
         )
-        summed = lax.psum(partial_sum, "feat")
+        summed = jnp.sum(lax.all_gather(partial_sum, "feat"), axis=0)
         return summed.reshape(-1, classes)
 
     def evaluate(row_data, weights_bf, adversary, counts):

time: 851 us -> 741 us (0.87)
  waiting for transfers between devices: 518 us -> 410 us
    psum x7 -> x0, waiting for transfers between devices: 220 us -> none  [total_logits(): summed = lax.psum(partial_sum, 'feat')]
    all_gather x0 -> x7, waiting for transfers between devices: none -> 107 us  [total_logits(): summed = jnp.sum(lax.all_gather(partial_sum, 'feat'), axis=0)]
    reduce_sum x0 -> x7, other arithmetic: none -> 9.16 us  [total_logits(): summed = jnp.sum(lax.all_gather(partial_sum, 'feat'), axis=0)]
where the time goes in v1:
time: 741 us; the launch traced here: 732 us
  waiting for transfers between devices  410 us (55%)
  local copies, waits for them, and re-layouts  135 us (18%)
  matrix products  98.8 us (13%)
  other arithmetic  36.5 us (5%)
  blocking collectives  35.9 us (5%)
  between operations  14.7 us (2%)
    psum x6, waiting for transfers between devices, advance(): grad_total = lax.psum(grad_local, 'samp')  303 us
    all_gather x7, waiting for transfers between devices, total_logits(): summed = jnp.sum(lax.all_gather(partial_sum, 'feat'), axis=0)  107 us
    reshape x6, local copies, waits for them, and re-layouts, evaluate(): grad_tiles = grad_tiles.reshape(blocks_here * per_row, block_size * classes)  47.3 us
    dot_general x6, local copies, waits for them, and re-layouts, evaluate(): jnp.einsum('rbij,ric->rbjc', x_rows, dz_blocks, preferred_element_type=jn...  41.4 us
    psum x3, blocking collectives, evaluate(): loss = lax.psum(local_loss, 'samp') / counts  35.9 us
    reshape x12, local copies, waits for them, and re-layouts, evaluate(): return (loss, grad_local.reshape(feat_rows, classes))  34.1 us
    dot_general x7, matrix products, total_logits(): jnp.einsum('rbij,rbjc->ric', x_rows, tiles, preferred_element_type=jnp.fl...  32.9 us
    dot_general x6, matrix products, evaluate(): jnp.einsum('rbij,ric->rbjc', x_rows, dz_blocks, preferred_element_type=jn...  29.2 us
  transfers between devices with their start and end apart: 13, of which 13 were waited for; matrix products, arithmetic and copies ran while one was open for 1% of the time, Pallas kernels for 0%

profile of v1, /device:TPU:0, one launch (start us, length us, event | category | flops | bytes accessed | tf_op | source)
XLA Modules:
  0.0 731.8 jit_solution(494705189807476659)
XLA Ops:
  10.5 4.4 convolution_bitcast_fusion.12
  16.2 18.4 %all-gather.15.cloned.1.call-done = f32[32,128,64]{1,2,0:T(8,128)} async-done(((f32[8,128,64]{1,2,0:T(8,128)}), f32[32,128,64]{1,2,0:T(8,128)}) %all-gather.15.cloned.1.call-update) | async-done | bytes 1048592 | tf_op jit(solution)/shard_map/all_gather | solution.py:40
  36.0 4.9 convolution_bitcast_fusion.5
  40.9 6.9 copy.130
  47.8 7.9 %reshape.440 = f32[128,8192]{1,0:T(8,128)} reshape(f32[8,16,128,64]{3,2,1,0:T(8,128)} %copy.130) | data formatting | bytes 8388608 | tf_op jit(solution)/shard_map/reshape | solution.py:60
  55.7 3.8 fusion.69
  59.5 2.2 reshape.441
  61.7 3.2 copy.131
  64.9 51.9 %all-reduce.10.cloned.1.call-done = f32[4096,64]{0,1:T(8,128)} async-done(((f32[4096,64]{0,1:T(8,128)}), f32[4096,64]{0,1:T(8,128)}) %all-reduce.10.cloned.1.call-update) | async-done | bytes 1048592 | tf_op jit(solution)/shard_map/psum | solution.py:66
  118.2 2.2 gather_fusion.1
  120.4 5.1 convolution_bitcast_fusion.11
  125.6 16.2 %all-gather.17.cloned.1.call-done = f32[32,128,64]{1,2,0:T(8,128)} async-done(((f32[8,128,64]{1,2,0:T(8,128)}), f32[32,128,64]{1,2,0:T(8,128)}) %all-gather.17.cloned.1.call-update) | async-done | bytes 1048592 | tf_op jit(solution)/shard_map/all_gather | solution.py:40
  144.1 12.2 %all-reduce.2 = (f32[8]{0:T(128)S(1)}, f32[8]{0:T(128)S(1)}) all-reduce(f32[8]{0:T(128)S(1)} %convolution_bitcast_fusion.21, f32[8]{0:T(128)S(1)} %convolution_bitcast_fusion.20), channel_id=1, replica_groups=mesh['groups'=2,'samp'=4,'feat'=4] {'samp'}, use_global_device_ids=true, to_apply=%region_5.0 | all-reduce | flops 16 | bytes 128 | tf_op jit(solution)/shard_map/psum | solution.py:52
  156.9 2.0 fusion.117
  160.7 4.9 convolution_bitcast_fusion.4
  165.6 6.9 copy.133
  172.5 7.9 %reshape.443 = f32[128,8192]{1,0:T(8,128)} reshape(f32[8,16,128,64]{3,2,1,0:T(8,128)} %copy.133) | data formatting | bytes 8388608 | tf_op jit(solution)/shard_map/reshape | solution.py:60
  180.4 3.8 fusion.68
  184.2 2.2 reshape.444
  186.4 3.2 copy.134
  189.6 49.2 %all-reduce.12.cloned.1.call-done = f32[4096,64]{0,1:T(8,128)} async-done(((f32[4096,64]{0,1:T(8,128)}), f32[4096,64]{0,1:T(8,128)}) %all-reduce.12.cloned.1.call-update) | async-done | bytes 1048592 | tf_op jit(solution)/shard_map/psum | solution.py:66
  240.2 2.2 gather_fusion.2
  242.4 5.1 convolution_bitcast_fusion.10
  249.6 14.2 %all-gather.19.cloned.1.call-done = f32[32,128,64]{1,2,0:T(8,128)} async-done(((f32[8,128,64]{1,2,0:T(8,128)}), f32[32,128,64]{1,2,0:T(8,128)}) %all-gather.19.cloned.1.call-update) | async-done | bytes 1048592 | tf_op jit(solution)/shard_map/all_gather | solution.py:40
  265.2 4.9 convolution_bitcast_fusion.3
  270.0 6.9 copy.136
  276.9 7.9 %reshape.447 = f32[128,8192]{1,0:T(8,128)} reshape(f32[8,16,128,64]{3,2,1,0:T(8,128)} %copy.136) | data formatting | bytes 8388608 | tf_op jit(solution)/shard_map/reshape | solution.py:60
  284.8 4.8 fusion.67
  289.6 3.2 reshape.448
  292.8 3.2 copy.137
  296.3 51.8 %all-reduce.14.cloned.1.call-done = f32[4096,64]{0,1:T(8,128)} async-done(((f32[4096,64]{0,1:T(8,128)}), f32[4096,64]{0,1:T(8,128)}) %all-reduce.14.cloned.1.call-update) | async-done | bytes 1048592 | tf_op jit(solution)/shard_map/psum | solution.py:66
  349.4 2.2 gather_fusion.3
  351.6 5.1 convolution_bitcast_fusion.9
  356.7 16.2 %all-gather.21.cloned.1.call-done = f32[32,128,64]{1,2,0:T(8,128)} async-done(((f32[8,128,64]{1,2,0:T(8,128)}), f32[32,128,64]{1,2,0:T(8,128)}) %all-gather.21.cloned.1.call-update) | async-done | bytes 1048592 | tf_op jit(solution)/shard_map/all_gather | solution.py:40
  375.2 11.7 %all-reduce.1 = (f32[8]{0:T(128)S(1)}, f32[8]{0:T(128)S(1)}) all-reduce(f32[8]{0:T(128)S(1)} %convolution_bitcast_fusion.19, f32[8]{0:T(128)S(1)} %convolution_bitcast_fusion.18), channel_id=1, replica_groups=mesh['groups'=2,'samp'=4,'feat'=4] {'samp'}, use_global_device_ids=true, to_apply=%region_23.0 | all-reduce | flops 16 | bytes 128 | tf_op jit(solution)/shard_map/psum | solution.py:52
  392.4 4.9 convolution_bitcast_fusion.2
  397.3 6.9 copy.139
  404.2 7.9 %reshape.450 = f32[128,8192]{1,0:T(8,128)} reshape(f32[8,16,128,64]{3,2,1,0:T(8,128)} %copy.139) | data formatting | bytes 8388608 | tf_op jit(solution)/shard_map/reshape | solution.py:60
  412.1 4.8 fusion.66
  416.9 3.1 reshape.451
  420.0 3.2 copy.140
  423.2 49.2 %all-reduce.16.cloned.1.call-done = f32[4096,64]{0,1:T(8,128)} async-done(((f32[4096,64]{0,1:T(8,128)}), f32[4096,64]{0,1:T(8,128)}) %all-reduce.16.cloned.1.call-update) | async-done | bytes 1048592 | tf_op jit(solution)/shard_map/psum | solution.py:66
  472.4 2.5 convert_bitcast_fusion
  476.0 4.4 convolution_bitcast_fusion.8
  483.9 12.8 %all-gather.23.cloned.1.call-done = f32[32,128,64]{1,2,0:T(8,128)} async-done(((f32[8,128,64]{1,2,0:T(8,128)}), f32[32,128,64]{1,2,0:T(8,128)}) %all-gather.23.cloned.1.call-update) | async-done | bytes 1048592 | tf_op jit(solution)/shard_map/all_gather | solution.py:40
  498.2 4.9 convolution_bitcast_fusion.1
  503.0 6.9 copy.142
  509.9 7.9 %reshape.454 = f32[128,8192]{1,0:T(8,128)} reshape(f32[8,16,128,64]{3,2,1,0:T(8,128)} %copy.142) | data formatting | bytes 8388608 | tf_op jit(solution)/shard_map/reshape | solution.py:60
  517.8 3.8 fusion.65
  521.6 2.2 reshape.455
  523.8 3.2 copy.143
  527.1 51.9 %all-reduce.18.cloned.1.call-done = f32[4096,64]{0,1:T(8,128)} async-done(((f32[4096,64]{0,1:T(8,128)}), f32[4096,64]{0,1:T(8,128)}) %all-reduce.18.cloned.1.call-update) | async-done | bytes 1048592 | tf_op jit(solution)/shard_map/psum | solution.py:66
  581.3 4.4 convolution_bitcast_fusion.7
  585.8 16.2 %all-gather.25.cloned.1.call-done = f32[32,128,64]{1,2,0:T(8,128)} async-done(((f32[8,128,64]{1,2,0:T(8,128)}), f32[32,128,64]{1,2,0:T(8,128)}) %all-gather.25.cloned.1.call-update) | async-done | bytes 1048592 | tf_op jit(solution)/shard_map/all_gather | solution.py:40
  604.4 11.9 %all-reduce = (f32[8]{0:T(128)S(1)}, f32[8]{0:T(128)S(1)}) all-reduce(f32[8]{0:T(128)S(1)} %convolution_bitcast_fusion.17, f32[8]{0:T(128)S(1)} %convolution_bitcast_fusion.16), channel_id=1, replica_groups=mesh['groups'=2,'samp'=4,'feat'=4] {'samp'}, use_global_device_ids=true, to_apply=%region_40.0 | all-reduce | flops 16 | bytes 128 | tf_op jit(solution)/shard_map/psum | solution.py:52
  621.8 4.9 convolution_bitcast_fusion
  626.7 6.9 copy.145
  633.6 7.9 %reshape.457 = f32[128,8192]{1,0:T(8,128)} reshape(f32[8,16,128,64]{3,2,1,0:T(8,128)} %copy.145) | data formatting | bytes 8388608 | tf_op jit(solution)/shard_map/reshape | solution.py:60
  641.5 3.8 fusion.64
  645.3 2.2 reshape.458
  647.5 3.2 copy.146
  650.7 49.2 %all-reduce.20.cloned.1.call-done = f32[4096,64]{0,1:T(8,128)} async-done(((f32[4096,64]{0,1:T(8,128)}), f32[4096,64]{0,1:T(8,128)}) %all-reduce.20.cloned.1.call-update) | async-done | bytes 1048592 | tf_op jit(solution)/shard_map/psum | solution.py:66
  702.3 4.4 convolution_bitcast_fusion.6
  709.8 13.2 %all-gather.27.cloned.1.call-done = f32[32,128,64]{1,2,0:T(8,128)} async-done(((f32[8,128,64]{1,2,0:T(8,128)}), f32[32,128,64]{1,2,0:T(8,128)}) %all-gather.27.cloned.1.call-update) | async-done | bytes 1048592 | tf_op jit(solution)/shard_map/all_gather | solution.py:40
  (135 shorter events, 50.2 us)
Async XLA Ops:
  7.2 8.2 %copy-start = (s32[4096]{0:T(1024)S(1)}, s32[4096]{0:T(1024)}, u32[]{:S(2)}) copy-start(s32[4096]{0:T(1024)} %param.8) | copy-start | bytes 49156
  7.2 27.4 %all-gather.15.cloned.1.call-start = ((), (), s32[]{:S(2)}) async-start(), calls=%async_computation.6 | async-start | bytes 1310720 | tf_op jit(solution)/shard_map/all_gather | solution.py:40
  10.5 4.5 copy-start.7
  10.5 4.9 copy-start.6
  15.0 101.9 %all-reduce.10.cloned.1.call-start = ((), (), s32[]{:S(2)}) async-start(), calls=%async_computation | async-start | bytes 2097152 | tf_op jit(solution)/shard_map/psum | solution.py:66
  59.5 57.4 %copy-start.2 = (f32[4096,64]{0,1:T(8,128)S(1)}, f32[4096,64]{0,1:T(8,128)}, u32[]{:S(2)}) copy-start(f32[4096,64]{0,1:T(8,128)} %param.11) | copy-start | bytes 3145732
  64.9 76.9 %all-gather.17.cloned.1.call-start = ((), (), s32[]{:S(2)}) async-start(), calls=%async_computation.7 | async-start | bytes 1310720 | tf_op jit(solution)/shard_map/all_gather | solution.py:40
  125.5 113.3 %all-reduce.12.cloned.1.call-start = ((), (), s32[]{:S(2)}) async-start(), calls=%async_computation.1 | async-start | bytes 2097152 | tf_op jit(solution)/shard_map/psum | solution.py:66
  189.6 74.1 %all-gather.19.cloned.1.call-start = ((), (), s32[]{:S(2)}) async-start(), calls=%async_computation.8 | async-start | bytes 1310720 | tf_op jit(solution)/shard_map/all_gather | solution.py:40
  247.4 100.6 %all-reduce.14.cloned.1.call-start = ((), (), s32[]{:S(2)}) async-start(), calls=%async_computation.2 | async-start | bytes 2097152 | tf_op jit(solution)/shard_map/psum | solution.py:66
  289.6 58.4 %copy-start.3 = (f32[4096,64]{0,1:T(8,128)S(1)}, f32[4096,64]{0,1:T(8,128)}, u32[]{:S(2)}) copy-start(f32[4096,64]{0,1:T(8,128)} %all-reduce.12.cloned.1.call-done) | copy-start | bytes 3145732
  296.0 76.9 %all-gather.21.cloned.1.call-start = ((), (), s32[]{:S(2)}) async-start(), calls=%async_computation.9 | async-start | bytes 1310720 | tf_op jit(solution)/shard_map/all_gather | solution.py:40
  356.7 115.7 %all-reduce.16.cloned.1.call-start = ((), (), s32[]{:S(2)}) async-start(), calls=%async_computation.3 | async-start | bytes 2097152 | tf_op jit(solution)/shard_map/psum | solution.py:66
  423.2 73.5 %all-gather.23.cloned.1.call-start = ((), (), s32[]{:S(2)}) async-start(), calls=%async_computation.10 | async-start | bytes 1310720 | tf_op jit(solution)/shard_map/all_gather | solution.py:40
  480.4 98.6 %all-reduce.18.cloned.1.call-start = ((), (), s32[]{:S(2)}) async-start(), calls=%async_computation.4 | async-start | bytes 2097152 | tf_op jit(solution)/shard_map/psum | solution.py:66
  521.6 57.4 %copy-start.4 = (f32[4096,64]{0,1:T(8,128)S(1)}, f32[4096,64]{0,1:T(8,128)}, u32[]{:S(2)}) copy-start(f32[4096,64]{0,1:T(8,128)} %get-tuple-element.29) | copy-start | bytes 3145732
  527.0 75.0 %all-gather.25.cloned.1.call-start = ((), (), s32[]{:S(2)}) async-start(), calls=%async_computation.11 | async-start | bytes 1310720 | tf_op jit(solution)/shard_map/all_gather | solution.py:40
  585.8 114.1 %all-reduce.20.cloned.1.call-start = ((), (), s32[]{:S(2)}) async-start(), calls=%async_computation.5 | async-start | bytes 2097152 | tf_op jit(solution)/shard_map/psum | solution.py:66
  645.3 54.6 %copy-start.5 = (f32[4096,64]{0,1:T(8,128)S(1)}, f32[4096,64]{0,1:T(8,128)}, u32[]{:S(2)}) copy-start(f32[4096,64]{0,1:T(8,128)} %get-tuple-element.29) | copy-start | bytes 3145732
  650.7 72.3 %all-gather.27.cloned.1.call-start = ((), (), s32[]{:S(2)}) async-start(), calls=%async_computation.12 | async-start | bytes 1310720 | tf_op jit(solution)/shard_map/all_gather | solution.py:40
  702.3 22.8 %copy-start.1 = (s32[4096]{0:T(1024)S(1)}, s32[4096]{0:T(1024)}, u32[]{:S(2)}) copy-start(s32[4096]{0:T(1024)} %param.8) | copy-start | bytes 49156
Sparse Core Ops, SparseCore 0:
  15.1 19.4 all-gather.14
  65.0 51.8 all-reduce.9
  125.6 16.0 all-gather.16
  189.7 49.0 all-reduce.11
  247.6 16.0 all-gather.18
  296.1 51.8 all-reduce.13
  356.8 16.1 all-gather.20
  423.3 49.0 all-reduce.15
  480.6 16.0 all-gather.22
  527.1 51.8 all-reduce.17
  585.9 16.1 all-gather.24
  650.8 49.0 all-reduce.19
  706.8 16.0 all-gather.26
